TPU v7x, 32 devices: a whole 2x2x4 slice. The times are simulated.
32 devices in a mesh: seq: 8 (over y, x, core), seg: 4 (over z).
Axes of the slice: x: 2, y: 2, z: 4, core: 2. Of those that a mesh axis runs over, the one named last changes fastest.
Arguments:
- query_rows: bfloat16 [4, 2048, 4, 128], P('seg', 'seq'), may hold values from -6 to 6
- key_rows: bfloat16 [4, 2048, 2, 4, 128], P('seg', 'seq'), may hold values from -6 to 6
- value_rows: bfloat16 [4, 2048, 2, 4, 128], P('seg', 'seq'), may hold values from -6 to 6
- out_gain: float32 [4, 128], replicated, may hold values from 0.5 to 1.5
- initial_state: float32 [4, 128, 128], replicated, may hold values from -24 to 24
Outputs:
- normed_out: bfloat16 [4, 2048, 4, 128], P('seg', 'seq')
All inputs are finite; a program needn't handle non-finite values.
Results may differ from a plain program's by a relative error of at most 0.004.
Values sent between devices are 32-bit elements; how exact they have to be, the bound alone decides.
A program may use at most 128 MiB of HBM per device.

v0:
```python
import functools

import jax
import jax.numpy as jnp
from jax import lax
from jax.experimental import pallas as pl
from jax.experimental.pallas import tpu as pltpu
from jax.sharding import PartitionSpec as P

F32 = jnp.float32
BF16 = jnp.bfloat16
REFL = 2
BLK = 128
SUB = 16
LANES = 128
MESH = pl.DeviceIdType.MESH


def dot(a, b):
    return lax.dot_general(a, b, (((1,), (0,)), ((), ())), preferred_element_type=F32)


def dot_bt(a, b):
    return lax.dot_general(a, b, (((1,), (1,)), ((), ())), preferred_element_type=F32)


def dot_at(a, b):
    return lax.dot_general(a, b, (((0,), (0,)), ((), ())), preferred_element_type=F32)


def split(x):
    high = x.astype(BF16)
    return high, (x - high.astype(F32)).astype(BF16)


def dot3(a, b):
    ah, al = a
    bh, bl = b
    rows, width = ah.shape[0], bh.shape[1]
    both = jnp.concatenate([ah, al], 0)
    if width <= LANES:
        full = dot(both, jnp.concatenate([bh, bl], 1))
        return full[:rows, :width] + (full[:rows, width:] + full[rows:, :width])
    full = dot(both, bh)
    return full[:rows] + (full[rows:] + dot(ah, bl))


def dot2(a, exact):
    rows = a[0].shape[0]
    full = dot(jnp.concatenate(a, 0), exact)
    return full[:rows] + full[rows:]


def iota(shape, axis):
    return lax.broadcasted_iota(jnp.int32, shape, axis)


def grouped(x, size, odd):
    return [x[g * size : (g + 1) * size] for g in range(odd, x.shape[0] // size, 2)]


def factors(first, per, heads, nblk, kf, vf, dsc, nsc, kb, scaled_hi, scaled_lo, before, pair):
    dk = kf.shape[1]
    row, col = iota((BLK, BLK), 0), iota((BLK, BLK), 1)
    eye = row == col
    lane = iota((SUB, BLK), 1)
    count = per * nblk

    keys, lowers, rcols, rrows = [], [], [], []
    for n in range(count):
        h, c = n // nblk, n % nblk
        key = kf[pl.ds(c * BLK * heads + first + h, BLK, stride=heads), :].astype(BF16)
        kb[first + h, c] = key
        gram = dot_bt(key, key)
        diag = jnp.where(eye, gram, 0.0)
        rcol = lax.rsqrt(jnp.sum(diag, axis=1, keepdims=True) + 1e-6)
        rrow = lax.rsqrt(jnp.sum(diag, axis=0, keepdims=True) + 1e-6)
        lower = jnp.where(row > col, gram * (2.0 * rcol) * rrow, 0.0)
        packed = lower[:SUB]
        for g in range(1, BLK // SUB):
            packed = jnp.where(lane // SUB == g, lower[g * SUB : (g + 1) * SUB], packed)
        dsc[n * SUB : (n + 1) * SUB, :] = packed
        keys.append(key)
        lowers.append(lower)
        rcols.append(rcol)
        rrows.append(rrow)

    lane_c = iota((count, BLK), 1)
    solved = []
    for i in range(SUB):
        line = dsc[pl.ds(i, count, stride=SUB), :]
        total = jnp.where(lane_c % SUB == i, 1.0, 0.0)
        for j in range(i):
            factor = jnp.take_along_axis(line, (lane_c // SUB) * SUB + j, axis=1)
            total = total - factor * solved[j]
        solved.append(total)
        nsc[pl.ds(i, count, stride=SUB), :] = total

    inverses = []
    for n in range(count):
        packed = nsc[n * SUB : (n + 1) * SUB, :]
        inverses.append(
            jnp.concatenate(
                [jnp.where(lane // SUB == g, packed, 0.0) for g in range(BLK // SUB)], axis=0
            )
        )
    half = BLK // 2
    size = SUB
    while size < BLK:
        paired = iota((half, BLK), 1) // size == 2 * (iota((half, BLK), 0) // size)
        for n in range(count):
            inv = split(inverses[n])
            odd = jnp.concatenate(grouped(lowers[n], size, 1), 0)
            part = dot3(split(jnp.where(paired, odd, 0.0)), inv)
            blank = jnp.zeros((size, BLK), F32)
            spread = []
            for g in range(half // size):
                spread += [blank, part[g * size : (g + 1) * size]]
            own = tuple(jnp.concatenate(grouped(x, size, 1), 0) for x in inv)
            fill = dot3(own, split(jnp.concatenate(spread, 0)))
            even, odd = grouped(inverses[n], size, 0), grouped(inverses[n], size, 1)
            rows = []
            for g in range(half // size):
                rows += [even[g], odd[g] - fill[g * size : (g + 1) * size]]
            inverses[n] = jnp.concatenate(rows, 0)
        size *= 2

    for h in range(per):
        trans = add = None
        for c in range(nblk):
            n = h * nblk + c
            key, rcol, rrow = keys[n], rcols[n], rrows[n]
            value = vf[pl.ds(c * BLK * heads + first + h, BLK, stride=heads), :].astype(BF16)
            weights = dot2(split(inverses[n] * (2.0 * rrow)), key)
            updates = dot2(split(inverses[n] * 2.0), value)
            scaled = split(jnp.concatenate([weights, updates], axis=1) * rcol)
            scaled_hi[first + h, c] = scaled[0]
            scaled_lo[first + h, c] = scaled[1]
            moved = dot_at(key, scaled[0]) + dot_at(key, scaled[1])
            step_trans = jnp.where(eye, 1.0, 0.0) - moved[:, :dk]
            step_add = moved[:, dk:]
            if c == 0:
                trans, add = step_trans, step_add
            else:
                so_far = jnp.concatenate([trans, add], axis=1)
                before[first + h, c] = so_far
                after = dot3(split(step_trans), split(so_far))
                trans, add = after[:, :dk], after[:, dk:] + step_add
        pair[first + h, :, :dk] = trans
        pair[first + h, :, dk:] = add


def readers(h, heads, nblk, qf, kb, scaled_hi, scaled_lo, before, reach, base):
    dk = qf.shape[1]
    tok = BLK // REFL
    visible = iota((tok, BLK), 1) <= REFL * iota((tok, BLK), 0) + (REFL - 1)
    for c in range(nblk):
        query = qf[pl.ds(c * tok * heads + h, tok, stride=heads), :]
        scores = jnp.where(visible, dot_bt(query.astype(BF16), kb[h, c]), 0.0)
        read = dot3(split(scores), (scaled_hi[h, c], scaled_lo[h, c]))
        project = query - read[:, :dk]
        local = read[:, dk:]
        rows = slice(c * tok, (c + 1) * tok)
        if c == 0:
            reach[h, rows, :] = project
            base[h, rows, :] = local
        else:
            gone = dot3(split(project), split(before[h, c]))
            reach[h, rows, :] = gone[:, :dk]
            base[h, rows, :] = gone[:, dk:] + local


def kernel(
    seqs, segs, heads, per,
    q_ref, k_ref, v_ref, gain_ref, init_ref, out_ref,
    qf, kf, vf, dsc, nsc, kb, scaled_hi, scaled_lo, before, pair, reach, base,
    rx, prefix, outgoing, total, tree, zx, first_state, zstate, own_state, state,
    put_sem, got_sem, zput_sem, zgot_sem, sput_sem, sgot_sem,
):
    dk = init_ref.shape[1]
    dv = init_ref.shape[2]
    nblk = k_ref.shape[0] // (heads * BLK)
    span = seqs // heads
    me = lax.axis_index("seq")
    seg = lax.axis_index("seg")
    owner = lax.rem(me, span) == 0
    mine = me // span

    barrier = pltpu.get_barrier_semaphore()
    for d in range(1, seqs):
        pl.semaphore_signal(
            barrier, inc=1,
            device_id={"seq": lax.rem(me + d, seqs), "seg": seg}, device_id_type=MESH,
        )
    for d in range(1, segs):
        pl.semaphore_signal(
            barrier, inc=1,
            device_id={"seq": me, "seg": lax.rem(seg + d, segs)}, device_id_type=MESH,
        )

    def copy(src, dst, put, got, to_seq, to_seg):
        return pltpu.make_async_remote_copy(
            src_ref=src, dst_ref=dst, send_sem=put, recv_sem=got,
            device_id={"seq": to_seq, "seg": to_seg}, device_id_type=MESH,
        )

    def put(h):
        return copy(pair.at[h], rx.at[me], put_sem.at[h], got_sem.at[me], h * span, seg)

    def got(s):
        return copy(rx.at[s], rx.at[s], put_sem.at[0], got_sem.at[s], s, seg)

    def sput(s):
        return copy(outgoing.at[s], own_state.at[mine], sput_sem.at[s], sgot_sem.at[mine], s, seg)

    def sgot(h):
        return copy(outgoing.at[0], own_state.at[h], sput_sem.at[0], sgot_sem.at[h], h * span, seg)

    def zput(g):
        return copy(tree.at[seqs - 2], zx.at[seg], zput_sem.at[g], zgot_sem.at[seg], me, g)

    def zgot(g):
        return copy(tree.at[seqs - 2], zx.at[g], zput_sem.at[g], zgot_sem.at[g], me, g)

    def fput(g):
        return copy(first_state, zstate, zput_sem.at[g], zgot_sem.at[0], me, g)

    kf[...] = k_ref[...].astype(F32)
    vf[...] = v_ref[...].astype(F32)
    qf[...] = q_ref[...].astype(F32)

    def local(i, _):
        turn = lax.rem(i + 1 + mine // per, heads // per)
        factors(turn * per, per, heads, nblk, kf, vf, dsc, nsc, kb, scaled_hi, scaled_lo, before, pair)

        @pl.when(i == 0)
        def _():
            pl.semaphore_wait(barrier, seqs + segs - 2)

        for d in range(per):
            h = turn * per + d

            @pl.when(me != h * span)
            def _():
                put(h).start()

        return 0

    lax.fori_loop(0, heads // per, local, 0)

    def reading(h, _):
        readers(h, heads, nblk, qf, kb, scaled_hi, scaled_lo, before, reach, base)
        return 0

    lax.fori_loop(0, heads, reading, 0)

    @pl.when(owner)
    def _():
        total[:, :dk] = jnp.where(iota((dk, dk), 0) == iota((dk, dk), 1), 1.0, 0.0).astype(F32)
        total[:, dk:] = jnp.zeros((dk, dv), F32)
        rx[me] = pair[mine]

        def arrived(s, _):
            @pl.when(s != me)
            def _():
                got(s).wait_recv()

            return 0

        lax.fori_loop(0, seqs, arrived, 0)
        parts = [rx.at[s] for s in range(seqs)]
        slot = 0
        while len(parts) > 1:
            joined = []
            for early, late in zip(parts[::2], parts[1::2]):
                after = dot3(split(late[:, :dk]), split(early[...]))
                tree[slot, :, :dk] = after[:, :dk]
                tree[slot, :, dk:] = after[:, dk:] + late[:, dk:]
                joined.append(tree.at[slot])
                slot += 1
            parts = joined + (parts[-1:] if len(parts) % 2 else [])

        @pl.when(seg == 0)
        def _():
            whole = tree[seqs - 2]
            first_state[...] = dot3(split(whole[:, :dk]), split(init_ref[mine])) + whole[:, dk:]
            for g in range(1, segs):
                fput(g).start()

        for g in range(2, segs):

            @pl.when((seg > 0) & (seg < g))
            def _():
                zput(g).start()

        def one(s, _):
            so_far = total[...]
            prefix[s] = so_far
            after = dot3(split(rx[s, :, :dk]), split(so_far))
            total[:, :dk] = after[:, :dk]
            total[:, dk:] = after[:, dk:] + rx[s, :, dk:]
            return 0

        lax.fori_loop(0, seqs, one, 0)

    @pl.when(owner)
    def _():
        @pl.when(seg == 0)
        def _():
            state[...] = init_ref[mine]

        @pl.when(seg > 0)
        def _():
            fput(0).wait_recv()
            state[...] = zstate[...]

        for g in range(1, segs - 1):

            @pl.when(g < seg)
            def _():
                zgot(g).wait_recv()
                state[...] = dot3(split(zx[g, :, :dk]), split(state[...])) + zx[g, :, dk:]

        def give(k, _):
            s = lax.rem(2 * seqs - 2 - me + k, seqs)
            ready = dot3(split(prefix[s, :, :dk]), split(state[...])) + prefix[s, :, dk:]

            @pl.when(s != me)
            def _():
                outgoing[s] = ready
                sput(s).start()

            @pl.when(s == me)
            def _():
                own_state[mine] = ready

            return 0

        lax.fori_loop(0, seqs, give, 0)

    for h in range(heads):

        @pl.when(me != h * span)
        def _():
            sgot(h).wait_recv()

        read = dot3(split(reach[h]), split(own_state[h])) + base[h]
        scale = lax.rsqrt(jnp.mean(read * read, axis=-1, keepdims=True) + 1e-6)
        normed = read * scale * gain_ref[h : h + 1, :]
        qf[pl.ds(h, read.shape[0], stride=heads), :] = normed
    out_ref[...] = qf[...].astype(BF16)

    for h in range(heads):

        @pl.when(me != h * span)
        def _():
            put(h).wait_send()

    @pl.when(owner)
    def _():
        @pl.when(seg == 0)
        def _():
            for g in range(1, segs):
                fput(g).wait_send()

        for g in range(2, segs):

            @pl.when((seg > 0) & (seg < g))
            def _():
                zput(g).wait_send()

        def done(s, _):
            @pl.when(s != me)
            def _():
                sput(s).wait_send()

            return 0

        lax.fori_loop(0, seqs, done, 0)


def per_device(seqs, segs, query_rows, key_rows, value_rows, out_gain, initial_state):
    _, tokens, heads, dk = query_rows.shape
    dv = value_rows.shape[-1]
    steps = tokens * REFL
    nblk = steps // BLK
    per = 2
    count = per * nblk
    wide = dk + dv
    vmem = pl.BlockSpec(memory_space=pltpu.VMEM)
    dma = pltpu.SemaphoreType.DMA
    out = pl.pallas_call(
        functools.partial(kernel, seqs, segs, heads, per),
        in_specs=[vmem] * 5,
        out_specs=vmem,
        out_shape=jax.ShapeDtypeStruct((tokens * heads, dv), BF16),
        scratch_shapes=[
            pltpu.VMEM((tokens * heads, dk), F32),
            pltpu.VMEM((steps * heads, dk), F32),
            pltpu.VMEM((steps * heads, dv), F32),
            pltpu.VMEM((count * SUB, BLK), F32),
            pltpu.VMEM((count * SUB, BLK), F32),
            pltpu.VMEM((heads, nblk, BLK, dk), BF16),
            pltpu.VMEM((heads, nblk, BLK, wide), BF16),
            pltpu.VMEM((heads, nblk, BLK, wide), BF16),
            pltpu.VMEM((heads, nblk, dk, wide), F32),
            pltpu.VMEM((heads, dk, wide), F32),
            pltpu.VMEM((heads, tokens, dk), F32),
            pltpu.VMEM((heads, tokens, dv), F32),
            pltpu.VMEM((seqs, dk, wide), F32),
            pltpu.VMEM((seqs, dk, wide), F32),
            pltpu.VMEM((seqs, dk, dv), F32),
            pltpu.VMEM((dk, wide), F32),
            pltpu.VMEM((seqs - 1, dk, wide), F32),
            pltpu.VMEM((segs, dk, wide), F32),
            pltpu.VMEM((dk, dv), F32),
            pltpu.VMEM((dk, dv), F32),
            pltpu.VMEM((heads, dk, dv), F32),
            pltpu.VMEM((dk, dv), F32),
            dma((heads,)),
            dma((seqs,)),
            dma((segs,)),
            dma((segs,)),
            dma((seqs,)),
            dma((heads,)),
        ],
        compiler_params=pltpu.CompilerParams(collective_id=0, has_side_effects=True),
        name="delta_product",
    )(
        query_rows.reshape(tokens * heads, dk),
        key_rows.reshape(steps * heads, dk),
        value_rows.reshape(steps * heads, dv),
        out_gain,
        initial_state,
    )
    return out.reshape(1, tokens, heads, dv)


def solution(mesh):
    return jax.shard_map(
        functools.partial(per_device, mesh.shape["seq"], mesh.shape["seg"]),
        mesh=mesh,
        in_specs=(
            P("seg", "seq", None, None),
            P("seg", "seq", None, None, None),
            P("seg", "seq", None, None, None),
            P(),
            P(),
        ),
        out_specs=P("seg", "seq", None, None),
        check_vma=False,
    )
```

profile of v0, /device:TPU:25, one launch (start us, length us, event | category | flops | bytes accessed | tf_op | source)
XLA Modules:
  0.0 31.1 jit_solution(18433189318244627692)
XLA Ops:
  0.0 29.3 %delta_product.1 = bf16[1024,128]{1,0:T(8,128)(2,1)} custom-call(bf16[1024,128]{1,0:T(8,128)(2,1)} %bitcast.7, bf16[2048,128]{1,0:T(8,128)(2,1)} %bitcast.5, bf16[2048,128]{1,0:T(8,128)(2,1)} %bitcast.6, f32[4,128]{1,0:T(4,128)} %gain_ref.1, f32[4,128,128]{2,1,0:T(8,128)} %init_ref.1), custom_call_target="tpu_custom_call" | custom-call | tf_op jit(solution)/shard_map/delta_product/pallas_call | solution.py:392
  29.3 1.7 %copy.7 = bf16[1,256,4,128]{3,2,1,0:T(4,128)(2,1)} copy(bf16[1,256,4,128]{3,2,1,0:T(4,128)(2,1)} %bitcast.4) | data formatting | bytes 524288
where the time goes:
time: 31.2 us; the launch traced here: 31.1 us
  Pallas kernels  29.3 us (94%)
  local copies, waits for them, and re-layouts  1.74 us (6%)
    pallas_call x1, Pallas kernels, per_device(): pl.pallas_call(functools.partial(kernel, seqs, segs, heads, per), in_spec...  29.3 us
    unnamed x1, local copies, waits for them, and re-layouts  1.74 us

commit v1 on v0

--- a/solution.py
+++ b/solution.py
@@ -393,7 +393,7 @@
         functools.partial(kernel, seqs, segs, heads, per),
         in_specs=[vmem] * 5,
         out_specs=vmem,
-        out_shape=jax.ShapeDtypeStruct((tokens * heads, dv), BF16),
+        out_shape=pltpu.VMEM((tokens * heads, dv), BF16),
         scratch_shapes=[
             pltpu.VMEM((tokens * heads, dk), F32),
             pltpu.VMEM((steps * heads, dk), F32),

time: 31.2 us -> 29.5 us (0.946)
  local copies, waits for them, and re-layouts: 1.74 us -> 0.71 us
  Pallas kernels: 29.3 us -> 28.6 us
    unnamed x1, local copies, waits for them, and re-layouts: 1.74 us -> 0.71 us
    pallas_call x1, Pallas kernels: 29.3 us -> 28.6 us  [per_device(): pl.pallas_call(functools.partial(kernel, seqs, segs, heads, per), in_spec...]
where the time goes in v1:
time: 29.5 us; the launch traced here: 29.4 us
  Pallas kernels  28.6 us (97%)
  local copies, waits for them, and re-layouts  0.71 us (2%)
    pallas_call x1, Pallas kernels, per_device(): pl.pallas_call(functools.partial(kernel, seqs, segs, heads, per), in_spec...  28.6 us
    unnamed x1, local copies, waits for them, and re-layouts  0.71 us

profile of v1, /device:TPU:25, one launch (start us, length us, event | category | flops | bytes accessed | tf_op | source)
XLA Modules:
  0.0 29.4 jit_solution(17531974884685777104)
XLA Ops:
  0.0 28.6 %delta_product.1 = bf16[1024,128]{1,0:T(8,128)(2,1)S(1)} custom-call(bf16[1024,128]{1,0:T(8,128)(2,1)} %bitcast.7, bf16[2048,128]{1,0:T(8,128)(2,1)} %bitcast.5, bf16[2048,128]{1,0:T(8,128)(2,1)} %bitcast.6, f32[4,128]{1,0:T(4,128)} %gain_ref.1, f32[4,128,128]{2,1,0:T(8,128)} %init_ref.1), custom_call_target="tpu_custom_call" | custom-call | tf_op jit(solution)/shard_map/delta_product/pallas_call | solution.py:392
  28.6 0.7 %copy.7 = bf16[1,256,4,128]{3,2,1,0:T(4,128)(2,1)} copy(bf16[1,256,4,128]{3,2,1,0:T(4,128)(2,1)S(1)} %bitcast.4) | data formatting | bytes 524288

commit v2 on v1

--- a/solution.py
+++ b/solution.py
@@ -59,126 +59,154 @@
     return [x[g * size : (g + 1) * size] for g in range(odd, x.shape[0] // size, 2)]
 
 
-def factors(first, per, heads, nblk, kf, vf, dsc, nsc, kb, scaled_hi, scaled_lo, before, pair):
-    dk = kf.shape[1]
+def invert_level(inv, low, size):
+    half = BLK // 2
+    paired = iota((half, BLK), 1) // size == 2 * (iota((half, BLK), 0) // size)
+    high, rest = split(inv)
+    under = jnp.where(paired, jnp.concatenate(grouped(low, size, 1), 0), 0.0)
+    part = dot3(split(under), (high, rest))
+    blank = jnp.zeros((size, BLK), F32)
+    spread = []
+    for g in range(half // size):
+        spread += [blank, part[g * size : (g + 1) * size]]
+    own = tuple(jnp.concatenate(grouped(x, size, 1), 0) for x in (high, rest))
+    fill = dot3(own, split(jnp.concatenate(spread, 0)))
+    even, odd = grouped(inv, size, 0), grouped(inv, size, 1)
+    rows = []
+    for g in range(half // size):
+        rows += [even[g], odd[g] - fill[g * size : (g + 1) * size]]
+    return jnp.concatenate(rows, 0)
+
+
+def wide(x):
+    return jnp.concatenate(split(x), 1)
+
+
+def tall(x):
+    return jnp.concatenate(split(x), 0)
+
+
+def compose_split(left, right):
+    lh, ll = left
+    rh, rl = right
+    return dot(jnp.concatenate([lh, ll], 1), jnp.concatenate([rh, rh], 0)) + dot(lh, rl)
+
+
+def compose(left, right):
+    return compose_split(split(left), split(right))
+
+
+def grams(first, per, heads, nblk, kf, dsc, low, norm, kb):
     row, col = iota((BLK, BLK), 0), iota((BLK, BLK), 1)
     eye = row == col
     lane = iota((SUB, BLK), 1)
     count = per * nblk
-
-    keys, lowers, rcols, rrows = [], [], [], []
-    for n in range(count):
-        h, c = n // nblk, n % nblk
-        key = kf[pl.ds(c * BLK * heads + first + h, BLK, stride=heads), :].astype(BF16)
-        kb[first + h, c] = key
-        gram = dot_bt(key, key)
-        diag = jnp.where(eye, gram, 0.0)
-        rcol = lax.rsqrt(jnp.sum(diag, axis=1, keepdims=True) + 1e-6)
-        rrow = lax.rsqrt(jnp.sum(diag, axis=0, keepdims=True) + 1e-6)
-        lower = jnp.where(row > col, gram * (2.0 * rcol) * rrow, 0.0)
+    at = [(first + n // nblk, n % nblk) for n in range(count)]
+    keys = [kf[pl.ds(c * BLK * heads + h, BLK, stride=heads), :].astype(BF16) for h, c in at]
+    products = [dot_bt(key, key) for key in keys]
+    diags = [jnp.where(eye, gram, 0.0) for gram in products]
+    rcols = [lax.rsqrt(jnp.sum(diag, axis=1, keepdims=True) + 1e-6) for diag in diags]
+    rrows = [lax.rsqrt(jnp.sum(diag, axis=0, keepdims=True) + 1e-6) for diag in diags]
+    for n, (h, c) in enumerate(at):
+        kb[h, c] = keys[n]
+        norm[first * nblk + n] = rrows[n]
+        lower = jnp.where(row > col, products[n] * (2.0 * rcols[n] * rcols[n]), 0.0)
+        low[first * nblk + n] = lower
         packed = lower[:SUB]
         for g in range(1, BLK // SUB):
             packed = jnp.where(lane // SUB == g, lower[g * SUB : (g + 1) * SUB], packed)
-        dsc[n * SUB : (n + 1) * SUB, :] = packed
-        keys.append(key)
-        lowers.append(lower)
-        rcols.append(rcol)
-        rrows.append(rrow)
-
-    lane_c = iota((count, BLK), 1)
+        dsc[pl.ds(pl.multiple_of((first * nblk + n) * SUB, SUB), SUB), :] = packed
+
+
+def substitute(count, dsc, nsc):
+    lane = iota((count, BLK), 1)
     solved = []
     for i in range(SUB):
         line = dsc[pl.ds(i, count, stride=SUB), :]
-        total = jnp.where(lane_c % SUB == i, 1.0, 0.0)
+        total = jnp.where(lane % SUB == i, 1.0, 0.0)
         for j in range(i):
-            factor = jnp.take_along_axis(line, (lane_c // SUB) * SUB + j, axis=1)
+            factor = jnp.take_along_axis(line, (lane // SUB) * SUB + j, axis=1)
             total = total - factor * solved[j]
         solved.append(total)
         nsc[pl.ds(i, count, stride=SUB), :] = total
 
+
+def factors(first, per, heads, nblk, vf, nsc, low, norm, kb, scaled_hi, scaled_lo, before, pair):
+    dk = kb.shape[-1]
+    eye = iota((BLK, BLK), 0) == iota((BLK, BLK), 1)
+    lane = iota((SUB, BLK), 1)
     inverses = []
-    for n in range(count):
-        packed = nsc[n * SUB : (n + 1) * SUB, :]
+    base = first * nblk
+    for n in range(per * nblk):
+        packed = nsc[pl.ds(pl.multiple_of((base + n) * SUB, SUB), SUB), :]
         inverses.append(
             jnp.concatenate(
                 [jnp.where(lane // SUB == g, packed, 0.0) for g in range(BLK // SUB)], axis=0
             )
         )
-    half = BLK // 2
     size = SUB
     while size < BLK:
-        paired = iota((half, BLK), 1) // size == 2 * (iota((half, BLK), 0) // size)
-        for n in range(count):
-            inv = split(inverses[n])
-            odd = jnp.concatenate(grouped(lowers[n], size, 1), 0)
-            part = dot3(split(jnp.where(paired, odd, 0.0)), inv)
-            blank = jnp.zeros((size, BLK), F32)
-            spread = []
-            for g in range(half // size):
-                spread += [blank, part[g * size : (g + 1) * size]]
-            own = tuple(jnp.concatenate(grouped(x, size, 1), 0) for x in inv)
-            fill = dot3(own, split(jnp.concatenate(spread, 0)))
-            even, odd = grouped(inverses[n], size, 0), grouped(inverses[n], size, 1)
-            rows = []
-            for g in range(half // size):
-                rows += [even[g], odd[g] - fill[g * size : (g + 1) * size]]
-            inverses[n] = jnp.concatenate(rows, 0)
+        inverses = [invert_level(inv, low[base + n], size) for n, inv in enumerate(inverses)]
         size *= 2
 
+    count = per * nblk
+    at = [(first + n // nblk, n % nblk) for n in range(count)]
+    keys = [kb[h, c] for h, c in at]
+    keys = [jnp.concatenate([key, key], 0) for key in keys]
+    values = [vf[pl.ds(c * BLK * heads + h, BLK, stride=heads), :].astype(BF16) for h, c in at]
+    rrows = [norm[base + n] for n in range(count)]
+    doubled = [inv * (2.0 * rrow) for inv, rrow in zip(inverses, rrows)]
+    updates = [dot(wide(d), jnp.concatenate([v, v], 0)) for d, v in zip(doubled, values)]
+    weights = [dot(wide(d * rrow), key) for d, rrow, key in zip(doubled, rrows, keys)]
+    scaled = [split(jnp.concatenate([w, u], axis=1)) for w, u in zip(weights, updates)]
+    moved = [dot_at(key, jnp.concatenate(s, 0)) for key, s in zip(keys, scaled)]
+    for (h, c), s in zip(at, scaled):
+        scaled_hi[h, c] = s[0]
+        scaled_lo[h, c] = s[1]
+    unit = jnp.where(eye, 1.0, 0.0)
+    so_far = [
+        jnp.concatenate([unit - moved[h * nblk][:, :dk], moved[h * nblk][:, dk:]], axis=1)
+        for h in range(per)
+    ]
+    for c in range(1, nblk):
+        for h in range(per):
+            step = moved[h * nblk + c]
+            before[first + h, c] = so_far[h]
+            after = compose(unit - step[:, :dk], so_far[h])
+            so_far[h] = jnp.concatenate([after[:, :dk], after[:, dk:] + step[:, dk:]], axis=1)
     for h in range(per):
-        trans = add = None
-        for c in range(nblk):
-            n = h * nblk + c
-            key, rcol, rrow = keys[n], rcols[n], rrows[n]
-            value = vf[pl.ds(c * BLK * heads + first + h, BLK, stride=heads), :].astype(BF16)
-            weights = dot2(split(inverses[n] * (2.0 * rrow)), key)
-            updates = dot2(split(inverses[n] * 2.0), value)
-            scaled = split(jnp.concatenate([weights, updates], axis=1) * rcol)
-            scaled_hi[first + h, c] = scaled[0]
-            scaled_lo[first + h, c] = scaled[1]
-            moved = dot_at(key, scaled[0]) + dot_at(key, scaled[1])
-            step_trans = jnp.where(eye, 1.0, 0.0) - moved[:, :dk]
-            step_add = moved[:, dk:]
-            if c == 0:
-                trans, add = step_trans, step_add
-            else:
-                so_far = jnp.concatenate([trans, add], axis=1)
-                before[first + h, c] = so_far
-                after = dot3(split(step_trans), split(so_far))
-                trans, add = after[:, :dk], after[:, dk:] + step_add
-        pair[first + h, :, :dk] = trans
-        pair[first + h, :, dk:] = add
+        pair[first + h] = so_far[h]
 
 
 def readers(h, heads, nblk, qf, kb, scaled_hi, scaled_lo, before, reach, base):
     dk = qf.shape[1]
     tok = BLK // REFL
     visible = iota((tok, BLK), 1) <= REFL * iota((tok, BLK), 0) + (REFL - 1)
-    for c in range(nblk):
-        query = qf[pl.ds(c * tok * heads + h, tok, stride=heads), :]
-        scores = jnp.where(visible, dot_bt(query.astype(BF16), kb[h, c]), 0.0)
-        read = dot3(split(scores), (scaled_hi[h, c], scaled_lo[h, c]))
-        project = query - read[:, :dk]
-        local = read[:, dk:]
+    blocks = range(nblk)
+    queries = [qf[pl.ds(c * tok * heads + h, tok, stride=heads), :] for c in blocks]
+    scores = [dot_bt(queries[c].astype(BF16), kb[h, c]) for c in blocks]
+    scores = [split(jnp.where(visible, score, 0.0)) for score in scores]
+    reads = [compose_split(scores[c], (scaled_hi[h, c], scaled_lo[h, c])) for c in blocks]
+    gone = [split(query - read[:, :dk]) for query, read in zip(queries, reads)]
+    reach[h, :tok, :] = jnp.concatenate(gone[0], 1)
+    base[h, :tok, :] = reads[0][:, dk:]
+    for c in range(1, nblk):
         rows = slice(c * tok, (c + 1) * tok)
-        if c == 0:
-            reach[h, rows, :] = project
-            base[h, rows, :] = local
-        else:
-            gone = dot3(split(project), split(before[h, c]))
-            reach[h, rows, :] = gone[:, :dk]
-            base[h, rows, :] = gone[:, dk:] + local
+        moved = compose_split(gone[c], split(before[h, c]))
+        reach[h, rows, :] = wide(moved[:, :dk])
+        base[h, rows, :] = moved[:, dk:] + reads[c][:, dk:]
 
 
 def kernel(
     seqs, segs, heads, per,
-    q_ref, k_ref, v_ref, gain_ref, init_ref, out_ref,
-    qf, kf, vf, dsc, nsc, kb, scaled_hi, scaled_lo, before, pair, reach, base,
+    q_any, k_any, v_any, gain_any, init_any, out_ref,
+    q_ref, k_ref, v_ref, gain_ref, init_ref, in_sem,
+    qf, kf, vf, dsc, nsc, low, norm, kb, scaled_hi, scaled_lo, before, pair, reach, base,
     rx, prefix, outgoing, total, tree, zx, first_state, zstate, own_state, state,
     put_sem, got_sem, zput_sem, zgot_sem, sput_sem, sgot_sem,
 ):
-    dk = init_ref.shape[1]
-    dv = init_ref.shape[2]
+    dk = init_ref.shape[0]
+    dv = init_ref.shape[1]
     nblk = k_ref.shape[0] // (heads * BLK)
     span = seqs // heads
     me = lax.axis_index("seq")
@@ -186,6 +214,20 @@
     owner = lax.rem(me, span) == 0
     mine = me // span
 
+    loads = [
+        pltpu.make_async_copy(src, dst, in_sem.at[i])
+        for i, (src, dst) in enumerate(
+            [
+                (k_any, k_ref),
+                (v_any, v_ref),
+                (q_any, q_ref),
+                (gain_any, gain_ref),
+                (init_any.at[mine], init_ref),
+            ]
+        )
+    ]
+    for load in loads:
+        load.start()
     barrier = pltpu.get_barrier_semaphore()
     for d in range(1, seqs):
         pl.semaphore_signal(
@@ -225,13 +267,23 @@
     def fput(g):
         return copy(first_state, zstate, zput_sem.at[g], zgot_sem.at[0], me, g)
 
+    loads[0].wait()
     kf[...] = k_ref[...].astype(F32)
+
+    def gramming(i, _):
+        grams(i * per, per, heads, nblk, kf, dsc, low, norm, kb)
+        return 0
+
+    lax.fori_loop(0, heads // per, gramming, 0)
+    substitute(heads * nblk, dsc, nsc)
+    for load in loads[1:]:
+        load.wait()
     vf[...] = v_ref[...].astype(F32)
     qf[...] = q_ref[...].astype(F32)
 
     def local(i, _):
         turn = lax.rem(i + 1 + mine // per, heads // per)
-        factors(turn * per, per, heads, nblk, kf, vf, dsc, nsc, kb, scaled_hi, scaled_lo, before, pair)
+        factors(turn * per, per, heads, nblk, vf, nsc, low, norm, kb, scaled_hi, scaled_lo, before, pair)
 
         @pl.when(i == 0)
         def _():
@@ -283,11 +335,11 @@
         @pl.when(seg == 0)
         def _():
             whole = tree[seqs - 2]
-            first_state[...] = dot3(split(whole[:, :dk]), split(init_ref[mine])) + whole[:, dk:]
-            for g in range(1, segs):
+            first_state[...] = dot3(split(whole[:, :dk]), split(init_ref[...])) + whole[:, dk:]
+            for g in range(segs - 1, 0, -1):
                 fput(g).start()
 
-        for g in range(2, segs):
+        for g in range(segs - 1, 1, -1):
 
             @pl.when((seg > 0) & (seg < g))
             def _():
@@ -307,7 +359,7 @@
     def _():
         @pl.when(seg == 0)
         def _():
-            state[...] = init_ref[mine]
+            state[...] = init_ref[...]
 
         @pl.when(seg > 0)
         def _():
@@ -344,9 +396,14 @@
         def _():
             sgot(h).wait_recv()
 
-        read = dot3(split(reach[h]), split(own_state[h])) + base[h]
-        scale = lax.rsqrt(jnp.mean(read * read, axis=-1, keepdims=True) + 1e-6)
-        normed = read * scale * gain_ref[h : h + 1, :]
+    states = [split(own_state[h]) for h in range(heads)]
+    reads = [
+        dot(reach[h], jnp.concatenate([hi, hi], 0)) + dot(reach[h, :, :dk], lo) + base[h]
+        for h, (hi, lo) in enumerate(states)
+    ]
+    squares = [jnp.mean(read * read, axis=-1, keepdims=True) for read in reads]
+    for h, read in enumerate(reads):
+        normed = read * lax.rsqrt(squares[h] + 1e-6) * gain_ref[h : h + 1, :]
         qf[pl.ds(h, read.shape[0], stride=heads), :] = normed
     out_ref[...] = qf[...].astype(BF16)
 
@@ -385,27 +442,36 @@
     steps = tokens * REFL
     nblk = steps // BLK
     per = 2
-    count = per * nblk
+    count = heads * nblk
     wide = dk + dv
+    anywhere = pl.BlockSpec(memory_space=pl.ANY)
     vmem = pl.BlockSpec(memory_space=pltpu.VMEM)
     dma = pltpu.SemaphoreType.DMA
     out = pl.pallas_call(
         functools.partial(kernel, seqs, segs, heads, per),
-        in_specs=[vmem] * 5,
+        in_specs=[anywhere] * 5,
         out_specs=vmem,
         out_shape=pltpu.VMEM((tokens * heads, dv), BF16),
         scratch_shapes=[
+            pltpu.VMEM((tokens * heads, dk), BF16),
+            pltpu.VMEM((steps * heads, dk), BF16),
+            pltpu.VMEM((steps * heads, dv), BF16),
+            pltpu.VMEM((heads, dv), F32),
+            pltpu.VMEM((dk, dv), F32),
+            dma((5,)),
             pltpu.VMEM((tokens * heads, dk), F32),
             pltpu.VMEM((steps * heads, dk), F32),
             pltpu.VMEM((steps * heads, dv), F32),
             pltpu.VMEM((count * SUB, BLK), F32),
             pltpu.VMEM((count * SUB, BLK), F32),
+            pltpu.VMEM((count, BLK, BLK), F32),
+            pltpu.VMEM((count, 1, BLK), F32),
             pltpu.VMEM((heads, nblk, BLK, dk), BF16),
             pltpu.VMEM((heads, nblk, BLK, wide), BF16),
             pltpu.VMEM((heads, nblk, BLK, wide), BF16),
             pltpu.VMEM((heads, nblk, dk, wide), F32),
             pltpu.VMEM((heads, dk, wide), F32),
-            pltpu.VMEM((heads, tokens, dk), F32),
+            pltpu.VMEM((heads, tokens, 2 * dk), BF16),
             pltpu.VMEM((heads, tokens, dv), F32),
             pltpu.VMEM((seqs, dk, wide), F32),
             pltpu.VMEM((seqs, dk, wide), F32),

time: 29.5 us -> 27.7 us (0.939)
  the two profiles are of different devices: /device:TPU:25 before, /device:TPU:17 now
where the time goes in v2:
time: 27.7 us; the launch traced here: 27.5 us
  Pallas kernels  26.8 us (97%)
  local copies, waits for them, and re-layouts  0.71 us (3%)
    pallas_call x1, Pallas kernels, per_device(): pl.pallas_call(functools.partial(kernel, seqs, segs, heads, per), in_spec...  26.8 us
    unnamed x1, local copies, waits for them, and re-layouts  0.71 us

profile of v2, /device:TPU:17, one launch (start us, length us, event | category | flops | bytes accessed | tf_op | source)
XLA Modules:
  0.0 27.5 jit_solution(14726228928462209638)
XLA Ops:
  0.0 26.8 %delta_product.1 = bf16[1024,128]{1,0:T(8,128)(2,1)S(1)} custom-call(bf16[1024,128]{1,0:T(8,128)(2,1)} %bitcast.7, bf16[2048,128]{1,0:T(8,128)(2,1)} %bitcast.5, bf16[2048,128]{1,0:T(8,128)(2,1)} %bitcast.6, f32[4,128]{1,0:T(4,128)} %gain_any.1, f32[4,128,128]{2,1,0:T(8,128)} %init_any.1), custom_call_target="tpu_custom_call" | custom-call | tf_op jit(solution)/shard_map/delta_product/pallas_call | solution.py:450
  26.8 0.7 %copy.7 = bf16[1,256,4,128]{3,2,1,0:T(4,128)(2,1)} copy(bf16[1,256,4,128]{3,2,1,0:T(4,128)(2,1)S(1)} %bitcast.4) | data formatting | bytes 524288

commit v3 on v2

--- a/solution.py
+++ b/solution.py
@@ -10,6 +10,7 @@
 F32 = jnp.float32
 BF16 = jnp.bfloat16
 REFL = 2
+CORES = 2
 BLK = 128
 SUB = 16
 LANES = 128
@@ -131,7 +132,7 @@
         nsc[pl.ds(i, count, stride=SUB), :] = total
 
 
-def factors(first, per, heads, nblk, vf, nsc, low, norm, kb, scaled_hi, scaled_lo, before, pair):
+def factors(first, per, heads, nblk, vf, nsc, low, norm, kb, scaled_hi, scaled_lo, before, both, core):
     dk = kb.shape[-1]
     eye = iota((BLK, BLK), 0) == iota((BLK, BLK), 1)
     lane = iota((SUB, BLK), 1)
@@ -175,7 +176,7 @@
             after = compose(unit - step[:, :dk], so_far[h])
             so_far[h] = jnp.concatenate([after[:, :dk], after[:, dk:] + step[:, dk:]], axis=1)
     for h in range(per):
-        pair[first + h] = so_far[h]
+        both[core, first + h] = so_far[h]
 
 
 def readers(h, heads, nblk, qf, kb, scaled_hi, scaled_lo, before, reach, base):
@@ -197,22 +198,46 @@
         base[h, rows, :] = moved[:, dk:] + reads[c][:, dk:]
 
 
+def applied(step, state):
+    dk = step.shape[0]
+    return compose(step[:, :dk], state) + step[:, dk:]
+
+
+def joined(late, early):
+    dk = early.shape[0]
+    after = compose(late[:, :dk], early)
+    return jnp.concatenate([after[:, :dk], after[:, dk:] + late[:, dk:]], axis=1)
+
+
+def folding(h, both, reach, base):
+    dk = both.shape[2]
+    moved = compose_split((reach[h, :, :dk], reach[h, :, dk:]), split(both[0, h]))
+    reach[h] = wide(moved[:, :dk])
+    base[h] = base[h] + moved[:, dk:]
+
+
 def kernel(
     seqs, segs, heads, per,
     q_any, k_any, v_any, gain_any, init_any, out_ref,
     q_ref, k_ref, v_ref, gain_ref, init_ref, in_sem,
-    qf, kf, vf, dsc, nsc, low, norm, kb, scaled_hi, scaled_lo, before, pair, reach, base,
+    qf, kf, vf, dsc, nsc, low, norm, kb, scaled_hi, scaled_lo, before, both, merged, reach, base,
     rx, prefix, outgoing, total, tree, zx, first_state, zstate, own_state, state,
-    put_sem, got_sem, zput_sem, zgot_sem, sput_sem, sgot_sem,
+    mput_sem, mgot_sem, put_sem, got_sem, zput_sem, zgot_sem, sput_sem, sgot_sem, rput_sem, rgot_sem,
 ):
     dk = init_ref.shape[0]
     dv = init_ref.shape[1]
+    half = dk // CORES
     nblk = k_ref.shape[0] // (heads * BLK)
     span = seqs // heads
+    chips = seqs // CORES
     me = lax.axis_index("seq")
     seg = lax.axis_index("seg")
+    core = lax.rem(me, CORES)
+    chip = me // CORES
+    mate = me + 1 - 2 * core
     owner = lax.rem(me, span) == 0
     mine = me // span
+    mine_rows = pl.ds(pl.multiple_of(core * half, half), half)
 
     loads = [
         pltpu.make_async_copy(src, dst, in_sem.at[i])
@@ -246,23 +271,42 @@
             device_id={"seq": to_seq, "seg": to_seg}, device_id_type=MESH,
         )
 
+    def mput(h, c):
+        ref = both.at[c, h] if c == 0 else both.at[c, h, :half]
+        return copy(ref, ref, mput_sem.at[h], mgot_sem.at[h], mate, seg)
+
+    def for_core(action):
+        for c in range(CORES):
+
+            @pl.when(core == c)
+            def _():
+                action(c)
+
     def put(h):
-        return copy(pair.at[h], rx.at[me], put_sem.at[h], got_sem.at[me], h * span, seg)
-
-    def got(s):
-        return copy(rx.at[s], rx.at[s], put_sem.at[0], got_sem.at[s], s, seg)
+        return copy(
+            merged.at[h], rx.at[chip, mine_rows], put_sem.at[h], got_sem.at[chip, core], h * span, seg
+        )
+
+    def got(s, c):
+        ref = rx.at[s, pl.ds(c * half, half)]
+        return copy(ref, ref, put_sem.at[0], got_sem.at[s, c], s * CORES, seg)
 
     def sput(s):
-        return copy(outgoing.at[s], own_state.at[mine], sput_sem.at[s], sgot_sem.at[mine], s, seg)
+        return copy(
+            outgoing.at[s], own_state.at[mine], sput_sem.at[s], sgot_sem.at[mine], s * CORES, seg
+        )
 
     def sgot(h):
-        return copy(outgoing.at[0], own_state.at[h], sput_sem.at[0], sgot_sem.at[h], h * span, seg)
+        return copy(own_state.at[h], own_state.at[h], sput_sem.at[0], sgot_sem.at[h], h * span, seg)
+
+    def rput(h):
+        return copy(own_state.at[h], own_state.at[h], rput_sem.at[h], rgot_sem.at[h], mate, seg)
 
     def zput(g):
-        return copy(tree.at[seqs - 2], zx.at[seg], zput_sem.at[g], zgot_sem.at[seg], me, g)
+        return copy(tree.at[chips - 2], zx.at[seg], zput_sem.at[g], zgot_sem.at[seg], me, g)
 
     def zgot(g):
-        return copy(tree.at[seqs - 2], zx.at[g], zput_sem.at[g], zgot_sem.at[g], me, g)
+        return copy(tree.at[chips - 2], zx.at[g], zput_sem.at[g], zgot_sem.at[g], me, g)
 
     def fput(g):
         return copy(first_state, zstate, zput_sem.at[g], zgot_sem.at[0], me, g)
@@ -281,24 +325,50 @@
     vf[...] = v_ref[...].astype(F32)
     qf[...] = q_ref[...].astype(F32)
 
+    def group_of(i):
+        turn = lax.rem(i + 1 + mine // per, heads // per)
+        return turn, [turn * per + lax.rem(mine + 1 + d, per) for d in range(per)]
+
     def local(i, _):
-        turn = lax.rem(i + 1 + mine // per, heads // per)
-        factors(turn * per, per, heads, nblk, vf, nsc, low, norm, kb, scaled_hi, scaled_lo, before, pair)
+        turn, group = group_of(i)
+        factors(turn * per, per, heads, nblk, vf, nsc, low, norm, kb, scaled_hi, scaled_lo, before, both, core)
 
         @pl.when(i == 0)
         def _():
             pl.semaphore_wait(barrier, seqs + segs - 2)
 
-        for d in range(per):
-            h = turn * per + d
+        def exchange(c):
+            for h in group:
+                mput(h, c).start()
+
+        for_core(exchange)
+        return 0
+
+    lax.fori_loop(0, heads // per, local, 0)
+
+    def merging(i, _):
+        _, group = group_of(i)
+
+        def arrived(c):
+            for h in group:
+                mput(h, 1 - c).wait_recv()
+
+        for_core(arrived)
+        results = [joined(both[1, h, mine_rows], both[0, h]) for h in group]
+        for h, result in zip(group, results):
+            merged[h] = result
 
             @pl.when(me != h * span)
             def _():
                 put(h).start()
 
+            @pl.when(me == h * span)
+            def _():
+                rx[chip, mine_rows] = merged[h]
+
         return 0
 
-    lax.fori_loop(0, heads // per, local, 0)
+    lax.fori_loop(0, heads // per, merging, 0)
 
     def reading(h, _):
         readers(h, heads, nblk, qf, kb, scaled_hi, scaled_lo, before, reach, base)
@@ -306,57 +376,61 @@
 
     lax.fori_loop(0, heads, reading, 0)
 
+    @pl.when(core > 0)
+    def _():
+        def fold(h, _):
+            folding(h, both, reach, base)
+            return 0
+
+        lax.fori_loop(0, heads, fold, 0)
+
     @pl.when(owner)
     def _():
+        def arrived(s, _):
+            for c in range(CORES):
+
+                @pl.when(s * CORES + c != me)
+                def _():
+                    got(s, c).wait_recv()
+
+            return 0
+
+        lax.fori_loop(0, chips, arrived, 0)
+        parts = [rx.at[s] for s in range(chips)]
+        slot = 0
+        while len(parts) > 1:
+            pairs = list(zip(parts[::2], parts[1::2]))
+            results = [joined(late[...], early[...]) for early, late in pairs]
+            fresh = []
+            for result in results:
+                tree[slot] = result
+                fresh.append(tree.at[slot])
+                slot += 1
+            parts = fresh + (parts[-1:] if len(parts) % 2 else [])
+
+        @pl.when(seg == 0)
+        def _():
+            first_state[...] = applied(tree[chips - 2], init_ref[...])
+            for g in range(segs - 1, 0, -1):
+                fput(g).start()
+
+        for g in range(segs - 1, 1, -1):
+
+            @pl.when((seg > 0) & (seg < g))
+            def _():
+                zput(g).start()
+
         total[:, :dk] = jnp.where(iota((dk, dk), 0) == iota((dk, dk), 1), 1.0, 0.0).astype(F32)
         total[:, dk:] = jnp.zeros((dk, dv), F32)
-        rx[me] = pair[mine]
-
-        def arrived(s, _):
-            @pl.when(s != me)
-            def _():
-                got(s).wait_recv()
-
-            return 0
-
-        lax.fori_loop(0, seqs, arrived, 0)
-        parts = [rx.at[s] for s in range(seqs)]
-        slot = 0
-        while len(parts) > 1:
-            joined = []
-            for early, late in zip(parts[::2], parts[1::2]):
-                after = dot3(split(late[:, :dk]), split(early[...]))
-                tree[slot, :, :dk] = after[:, :dk]
-                tree[slot, :, dk:] = after[:, dk:] + late[:, dk:]
-                joined.append(tree.at[slot])
-                slot += 1
-            parts = joined + (parts[-1:] if len(parts) % 2 else [])
-
-        @pl.when(seg == 0)
-        def _():
-            whole = tree[seqs - 2]
-            first_state[...] = dot3(split(whole[:, :dk]), split(init_ref[...])) + whole[:, dk:]
-            for g in range(segs - 1, 0, -1):
-                fput(g).start()
-
-        for g in range(segs - 1, 1, -1):
-
-            @pl.when((seg > 0) & (seg < g))
-            def _():
-                zput(g).start()
 
         def one(s, _):
             so_far = total[...]
             prefix[s] = so_far
-            after = dot3(split(rx[s, :, :dk]), split(so_far))
-            total[:, :dk] = after[:, :dk]
-            total[:, dk:] = after[:, dk:] + rx[s, :, dk:]
+            total[...] = joined(rx[s], so_far)
             return 0
 
-        lax.fori_loop(0, seqs, one, 0)
-
-    @pl.when(owner)
-    def _():
+        lax.fori_loop(0, chips, one, 0)
+
         @pl.when(seg == 0)
         def _():
             state[...] = init_ref[...]
@@ -371,30 +445,43 @@
             @pl.when(g < seg)
             def _():
                 zgot(g).wait_recv()
-                state[...] = dot3(split(zx[g, :, :dk]), split(state[...])) + zx[g, :, dk:]
+                state[...] = applied(zx[g], state[...])
 
         def give(k, _):
-            s = lax.rem(2 * seqs - 2 - me + k, seqs)
-            ready = dot3(split(prefix[s, :, :dk]), split(state[...])) + prefix[s, :, dk:]
-
-            @pl.when(s != me)
+            s = lax.rem(2 * chips - 1 - chip + k, chips)
+            ready = applied(prefix[s], state[...])
+
+            @pl.when(s != chip)
             def _():
                 outgoing[s] = ready
                 sput(s).start()
 
-            @pl.when(s == me)
+            @pl.when(s == chip)
             def _():
                 own_state[mine] = ready
 
             return 0
 
-        lax.fori_loop(0, seqs, give, 0)
-
-    for h in range(heads):
-
-        @pl.when(me != h * span)
-        def _():
-            sgot(h).wait_recv()
+        lax.fori_loop(0, chips, give, 0)
+
+    @pl.when(core == 0)
+    def _():
+        def relay(k, _):
+            h = lax.rem(mine + (k // per) + (k % per) * (heads // per), heads)
+
+            @pl.when(me != h * span)
+            def _():
+                sgot(h).wait_recv()
+
+            rput(h).start()
+            return 0
+
+        lax.fori_loop(0, heads, relay, 0)
+
+    @pl.when(core > 0)
+    def _():
+        for h in range(heads):
+            rput(h).wait_recv()
 
     states = [split(own_state[h]) for h in range(heads)]
     reads = [
@@ -407,11 +494,21 @@
         qf[pl.ds(h, read.shape[0], stride=heads), :] = normed
     out_ref[...] = qf[...].astype(BF16)
 
+    def sent(c):
+        for h in range(heads):
+            mput(h, c).wait_send()
+
+    for_core(sent)
+
     for h in range(heads):
 
         @pl.when(me != h * span)
         def _():
             put(h).wait_send()
+
+        @pl.when(core == 0)
+        def _():
+            rput(h).wait_send()
 
     @pl.when(owner)
     def _():
@@ -427,13 +524,13 @@
                 zput(g).wait_send()
 
         def done(s, _):
-            @pl.when(s != me)
+            @pl.when(s != chip)
             def _():
                 sput(s).wait_send()
 
             return 0
 
-        lax.fori_loop(0, seqs, done, 0)
+        lax.fori_loop(0, chips, done, 0)
 
 
 def per_device(seqs, segs, query_rows, key_rows, value_rows, out_gain, initial_state):
@@ -444,6 +541,7 @@
     per = 2
     count = heads * nblk
     wide = dk + dv
+    chips = seqs // CORES
     anywhere = pl.BlockSpec(memory_space=pl.ANY)
     vmem = pl.BlockSpec(memory_space=pltpu.VMEM)
     dma = pltpu.SemaphoreType.DMA
@@ -470,24 +568,29 @@
             pltpu.VMEM((heads, nblk, BLK, wide), BF16),
             pltpu.VMEM((heads, nblk, BLK, wide), BF16),
             pltpu.VMEM((heads, nblk, dk, wide), F32),
-            pltpu.VMEM((heads, dk, wide), F32),
+            pltpu.VMEM((CORES, heads, dk, wide), F32),
+            pltpu.VMEM((heads, dk // CORES, wide), F32),
             pltpu.VMEM((heads, tokens, 2 * dk), BF16),
             pltpu.VMEM((heads, tokens, dv), F32),
-            pltpu.VMEM((seqs, dk, wide), F32),
-            pltpu.VMEM((seqs, dk, wide), F32),
-            pltpu.VMEM((seqs, dk, dv), F32),
+            pltpu.VMEM((chips, dk, wide), F32),
+            pltpu.VMEM((chips, dk, wide), F32),
+            pltpu.VMEM((chips, dk, dv), F32),
             pltpu.VMEM((dk, wide), F32),
-            pltpu.VMEM((seqs - 1, dk, wide), F32),
+            pltpu.VMEM((chips - 1, dk, wide), F32),
             pltpu.VMEM((segs, dk, wide), F32),
             pltpu.VMEM((dk, dv), F32),
             pltpu.VMEM((dk, dv), F32),
             pltpu.VMEM((heads, dk, dv), F32),
             pltpu.VMEM((dk, dv), F32),
             dma((heads,)),
-            dma((seqs,)),
+            dma((heads,)),
+            dma((heads,)),
+            dma((chips, CORES)),
             dma((segs,)),
             dma((segs,)),
-            dma((seqs,)),
+            dma((chips,)),
+            dma((heads,)),
+            dma((heads,)),
             dma((heads,)),
         ],
         compiler_params=pltpu.CompilerParams(collective_id=0, has_side_effects=True),

time: 27.7 us -> 27.3 us (0.986)
  Pallas kernels: 26.8 us -> 26.5 us
    pallas_call x1, Pallas kernels: 26.8 us -> 26.5 us  [per_device(): pl.pallas_call(functools.partial(kernel, seqs, segs, heads, per), in_spec...]
where the time goes in v3:
time: 27.3 us; the launch traced here: 27.2 us
  Pallas kernels  26.5 us (97%)
  local copies, waits for them, and re-layouts  0.71 us (3%)
    pallas_call x1, Pallas kernels, per_device(): pl.pallas_call(functools.partial(kernel, seqs, segs, heads, per), in_spec...  26.5 us
    unnamed x1, local copies, waits for them, and re-layouts  0.71 us

profile of v3, /device:TPU:17, one launch (start us, length us, event | category | flops | bytes accessed | tf_op | source)
XLA Modules:
  0.0 27.2 jit_solution(14579762863405447536)
XLA Ops:
  0.0 26.5 %delta_product.1 = bf16[1024,128]{1,0:T(8,128)(2,1)S(1)} custom-call(bf16[1024,128]{1,0:T(8,128)(2,1)} %bitcast.7, bf16[2048,128]{1,0:T(8,128)(2,1)} %bitcast.5, bf16[2048,128]{1,0:T(8,128)(2,1)} %bitcast.6, f32[4,128]{1,0:T(4,128)} %gain_any.1, f32[4,128,128]{2,1,0:T(8,128)} %init_any.1), custom_call_target="tpu_custom_call" | custom-call | tf_op jit(solution)/shard_map/delta_product/pallas_call | solution.py:548
  26.5 0.7 %copy.7 = bf16[1,256,4,128]{3,2,1,0:T(4,128)(2,1)} copy(bf16[1,256,4,128]{3,2,1,0:T(4,128)(2,1)S(1)} %bitcast.4) | data formatting | bytes 524288

commit v4 on v3

--- a/solution.py
+++ b/solution.py
@@ -60,12 +60,21 @@
     return [x[g * size : (g + 1) * size] for g in range(odd, x.shape[0] // size, 2)]
 
 
+def joined(late, early):
+    dk = early.shape[0]
+    after = compose(late[:, :dk], early)
+    return jnp.concatenate([after[:, :dk], after[:, dk:] + late[:, dk:]], axis=1)
+
+
 def invert_level(inv, low, size):
     half = BLK // 2
     paired = iota((half, BLK), 1) // size == 2 * (iota((half, BLK), 0) // size)
     high, rest = split(inv)
     under = jnp.where(paired, jnp.concatenate(grouped(low, size, 1), 0), 0.0)
-    part = dot3(split(under), (high, rest))
+    if 2 * size == BLK:
+        part = dot3(split(under[:, :size]), (high[:size], rest[:size]))
+    else:
+        part = dot3(split(under), (high, rest))
     blank = jnp.zeros((size, BLK), F32)
     spread = []
     for g in range(half // size):
@@ -132,7 +141,7 @@
         nsc[pl.ds(i, count, stride=SUB), :] = total
 
 
-def factors(first, per, heads, nblk, vf, nsc, low, norm, kb, scaled_hi, scaled_lo, before, both, core):
+def factors(first, per, heads, nblk, vf, nsc, low, norm, kb, steps, scaled_hi, scaled_lo, before, both, core):
     dk = kb.shape[-1]
     eye = iota((BLK, BLK), 0) == iota((BLK, BLK), 1)
     lane = iota((SUB, BLK), 1)
@@ -165,21 +174,22 @@
         scaled_hi[h, c] = s[0]
         scaled_lo[h, c] = s[1]
     unit = jnp.where(eye, 1.0, 0.0)
-    so_far = [
-        jnp.concatenate([unit - moved[h * nblk][:, :dk], moved[h * nblk][:, dk:]], axis=1)
-        for h in range(per)
-    ]
-    for c in range(1, nblk):
+    nodes = [jnp.concatenate([unit - m[:, :dk], m[:, dk:]], axis=1) for m in moved]
+    for n, (h, c) in enumerate(at):
+        if c & (c + 1):
+            steps[h, c] = nodes[n]
+    nodes = [nodes[h * nblk : (h + 1) * nblk] for h in range(per)]
+    reached = 1
+    while len(nodes[0]) > 1:
         for h in range(per):
-            step = moved[h * nblk + c]
-            before[first + h, c] = so_far[h]
-            after = compose(unit - step[:, :dk], so_far[h])
-            so_far[h] = jnp.concatenate([after[:, :dk], after[:, dk:] + step[:, dk:]], axis=1)
+            before[first + h, reached] = nodes[h][0]
+        nodes = [[joined(late, early) for early, late in zip(x[::2], x[1::2])] for x in nodes]
+        reached *= 2
     for h in range(per):
-        both[core, first + h] = so_far[h]
-
-
-def readers(h, heads, nblk, qf, kb, scaled_hi, scaled_lo, before, reach, base):
+        both[core, first + h] = nodes[h][0]
+
+
+def readers(h, heads, nblk, qf, kb, steps, scaled_hi, scaled_lo, before, reach, base):
     dk = qf.shape[1]
     tok = BLK // REFL
     visible = iota((tok, BLK), 1) <= REFL * iota((tok, BLK), 0) + (REFL - 1)
@@ -191,9 +201,11 @@
     gone = [split(query - read[:, :dk]) for query, read in zip(queries, reads)]
     reach[h, :tok, :] = jnp.concatenate(gone[0], 1)
     base[h, :tok, :] = reads[0][:, dk:]
+    so_far = None
     for c in range(1, nblk):
         rows = slice(c * tok, (c + 1) * tok)
-        moved = compose_split(gone[c], split(before[h, c]))
+        so_far = joined(steps[h, c - 1], so_far) if c & (c - 1) else before[h, c]
+        moved = compose_split(gone[c], split(so_far))
         reach[h, rows, :] = wide(moved[:, :dk])
         base[h, rows, :] = moved[:, dk:] + reads[c][:, dk:]
 
@@ -201,12 +213,6 @@
 def applied(step, state):
     dk = step.shape[0]
     return compose(step[:, :dk], state) + step[:, dk:]
-
-
-def joined(late, early):
-    dk = early.shape[0]
-    after = compose(late[:, :dk], early)
-    return jnp.concatenate([after[:, :dk], after[:, dk:] + late[:, dk:]], axis=1)
 
 
 def folding(h, both, reach, base):
@@ -220,7 +226,7 @@
     seqs, segs, heads, per,
     q_any, k_any, v_any, gain_any, init_any, out_ref,
     q_ref, k_ref, v_ref, gain_ref, init_ref, in_sem,
-    qf, kf, vf, dsc, nsc, low, norm, kb, scaled_hi, scaled_lo, before, both, merged, reach, base,
+    qf, kf, vf, dsc, nsc, low, norm, kb, steps, scaled_hi, scaled_lo, before, both, merged, reach, base,
     rx, prefix, outgoing, total, tree, zx, first_state, zstate, own_state, state,
     mput_sem, mgot_sem, put_sem, got_sem, zput_sem, zgot_sem, sput_sem, sgot_sem, rput_sem, rgot_sem,
 ):
@@ -238,6 +244,12 @@
     owner = lax.rem(me, span) == 0
     mine = me // span
     mine_rows = pl.ds(pl.multiple_of(core * half, half), half)
+
+    def near(first, second):
+        return (first != second) & ((first // 2 == second // 2) | (first % 2 == second % 2))
+
+    def relayed(h):
+        return jnp.logical_not(near(h * span // CORES, chip))
 
     loads = [
         pltpu.make_async_copy(src, dst, in_sem.at[i])
@@ -291,13 +303,13 @@
         ref = rx.at[s, pl.ds(c * half, half)]
         return copy(ref, ref, put_sem.at[0], got_sem.at[s, c], s * CORES, seg)
 
-    def sput(s):
+    def sput(s, c):
         return copy(
-            outgoing.at[s], own_state.at[mine], sput_sem.at[s], sgot_sem.at[mine], s * CORES, seg
+            outgoing.at[s], own_state.at[mine], sput_sem.at[s, c], sgot_sem.at[mine], s * CORES + c, seg
         )
 
     def sgot(h):
-        return copy(own_state.at[h], own_state.at[h], sput_sem.at[0], sgot_sem.at[h], h * span, seg)
+        return copy(own_state.at[h], own_state.at[h], sput_sem.at[0, 0], sgot_sem.at[h], h * span, seg)
 
     def rput(h):
         return copy(own_state.at[h], own_state.at[h], rput_sem.at[h], rgot_sem.at[h], mate, seg)
@@ -331,7 +343,7 @@
 
     def local(i, _):
         turn, group = group_of(i)
-        factors(turn * per, per, heads, nblk, vf, nsc, low, norm, kb, scaled_hi, scaled_lo, before, both, core)
+        factors(turn * per, per, heads, nblk, vf, nsc, low, norm, kb, steps, scaled_hi, scaled_lo, before, both, core)
 
         @pl.when(i == 0)
         def _():
@@ -371,7 +383,7 @@
     lax.fori_loop(0, heads // per, merging, 0)
 
     def reading(h, _):
-        readers(h, heads, nblk, qf, kb, scaled_hi, scaled_lo, before, reach, base)
+        readers(h, heads, nblk, qf, kb, steps, scaled_hi, scaled_lo, before, reach, base)
         return 0
 
     lax.fori_loop(0, heads, reading, 0)
@@ -454,7 +466,11 @@
             @pl.when(s != chip)
             def _():
                 outgoing[s] = ready
-                sput(s).start()
+                sput(s, 0).start()
+
+            @pl.when(near(s, chip))
+            def _():
+                sput(s, 1).start()
 
             @pl.when(s == chip)
             def _():
@@ -463,35 +479,50 @@
             return 0
 
         lax.fori_loop(0, chips, give, 0)
+
+    def ordered(k):
+        return lax.rem(mine + (k // per) + (k % per) * (heads // per), heads)
 
     @pl.when(core == 0)
     def _():
-        def relay(k, _):
-            h = lax.rem(mine + (k // per) + (k % per) * (heads // per), heads)
+        for k in range(heads):
+            h = ordered(k)
 
             @pl.when(me != h * span)
             def _():
                 sgot(h).wait_recv()
 
-            rput(h).start()
-            return 0
-
-        lax.fori_loop(0, heads, relay, 0)
-
-    @pl.when(core > 0)
-    def _():
-        for h in range(heads):
-            rput(h).wait_recv()
-
-    states = [split(own_state[h]) for h in range(heads)]
-    reads = [
-        dot(reach[h], jnp.concatenate([hi, hi], 0)) + dot(reach[h, :, :dk], lo) + base[h]
-        for h, (hi, lo) in enumerate(states)
-    ]
-    squares = [jnp.mean(read * read, axis=-1, keepdims=True) for read in reads]
-    for h, read in enumerate(reads):
-        normed = read * lax.rsqrt(squares[h] + 1e-6) * gain_ref[h : h + 1, :]
-        qf[pl.ds(h, read.shape[0], stride=heads), :] = normed
+            @pl.when(relayed(h))
+            def _():
+                rput(h).start()
+
+    def closing(i, _):
+        group = [ordered(i * 2 + d) for d in range(2)]
+
+        @pl.when(core > 0)
+        def _():
+            for h in group:
+
+                @pl.when(relayed(h))
+                def _():
+                    rput(h).wait_recv()
+
+                @pl.when(jnp.logical_not(relayed(h)))
+                def _():
+                    sgot(h).wait_recv()
+
+        states = [split(own_state[h]) for h in group]
+        reads = [
+            dot(reach[h], jnp.concatenate([hi, hi], 0)) + dot(reach[h, :, :dk], lo) + base[h]
+            for h, (hi, lo) in zip(group, states)
+        ]
+        squares = [jnp.mean(read * read, axis=-1, keepdims=True) for read in reads]
+        for h, read, square in zip(group, reads, squares):
+            normed = read * lax.rsqrt(square + 1e-6) * gain_ref[pl.ds(h, 1), :]
+            qf[pl.ds(h, read.shape[0], stride=heads), :] = normed
+        return 0
+
+    lax.fori_loop(0, heads // 2, closing, 0)
     out_ref[...] = qf[...].astype(BF16)
 
     def sent(c):
@@ -506,7 +537,7 @@
         def _():
             put(h).wait_send()
 
-        @pl.when(core == 0)
+        @pl.when((core == 0) & relayed(h))
         def _():
             rput(h).wait_send()
 
@@ -526,7 +557,11 @@
         def done(s, _):
             @pl.when(s != chip)
             def _():
-                sput(s).wait_send()
+                sput(s, 0).wait_send()
+
+            @pl.when(near(s, chip))
+            def _():
+                sput(s, 1).wait_send()
 
             return 0
 
@@ -565,6 +600,7 @@
             pltpu.VMEM((count, BLK, BLK), F32),
             pltpu.VMEM((count, 1, BLK), F32),
             pltpu.VMEM((heads, nblk, BLK, dk), BF16),
+            pltpu.VMEM((heads, nblk, dk, wide), F32),
             pltpu.VMEM((heads, nblk, BLK, wide), BF16),
             pltpu.VMEM((heads, nblk, BLK, wide), BF16),
             pltpu.VMEM((heads, nblk, dk, wide), F32),
@@ -588,7 +624,7 @@
             dma((chips, CORES)),
             dma((segs,)),
             dma((segs,)),
-            dma((chips,)),
+            dma((chips, CORES)),
             dma((heads,)),
             dma((heads,)),
             dma((heads,)),

time: 27.3 us -> 26.7 us (0.978)
  Pallas kernels: 26.5 us -> 25.8 us
    pallas_call x1, Pallas kernels: 26.5 us -> 25.8 us  [per_device(): pl.pallas_call(functools.partial(kernel, seqs, segs, heads, per), in_spec...]
where the time goes in v4:
time: 26.7 us; the launch traced here: 26.6 us
  Pallas kernels  25.8 us (97%)
  local copies, waits for them, and re-layouts  0.71 us (3%)
    pallas_call x1, Pallas kernels, per_device(): pl.pallas_call(functools.partial(kernel, seqs, segs, heads, per), in_spec...  25.8 us
    unnamed x1, local copies, waits for them, and re-layouts  0.71 us

profile of v4, /device:TPU:17, one launch (start us, length us, event | category | flops | bytes accessed | tf_op | source)
XLA Modules:
  0.0 26.6 jit_solution(12630671773914288180)
XLA Ops:
  0.0 25.8 %delta_product.1 = bf16[1024,128]{1,0:T(8,128)(2,1)S(1)} custom-call(bf16[1024,128]{1,0:T(8,128)(2,1)} %bitcast.7, bf16[2048,128]{1,0:T(8,128)(2,1)} %bitcast.5, bf16[2048,128]{1,0:T(8,128)(2,1)} %bitcast.6, f32[4,128]{1,0:T(4,128)} %gain_any.1, f32[4,128,128]{2,1,0:T(8,128)} %init_any.1), custom_call_target="tpu_custom_call" | custom-call | tf_op jit(solution)/shard_map/delta_product/pallas_call | solution.py:583
  25.9 0.7 %copy.7 = bf16[1,256,4,128]{3,2,1,0:T(4,128)(2,1)} copy(bf16[1,256,4,128]{3,2,1,0:T(4,128)(2,1)S(1)} %bitcast.4) | data formatting | bytes 524288

commit v5 on v4

--- a/solution.py
+++ b/solution.py
@@ -110,38 +110,44 @@
     row, col = iota((BLK, BLK), 0), iota((BLK, BLK), 1)
     eye = row == col
     lane = iota((SUB, BLK), 1)
-    count = per * nblk
-    at = [(first + n // nblk, n % nblk) for n in range(count)]
-    keys = [kf[pl.ds(c * BLK * heads + h, BLK, stride=heads), :].astype(BF16) for h, c in at]
-    products = [dot_bt(key, key) for key in keys]
-    diags = [jnp.where(eye, gram, 0.0) for gram in products]
-    rcols = [lax.rsqrt(jnp.sum(diag, axis=1, keepdims=True) + 1e-6) for diag in diags]
-    rrows = [lax.rsqrt(jnp.sum(diag, axis=0, keepdims=True) + 1e-6) for diag in diags]
+    at = [(first + n // nblk, n % nblk) for n in range(per * nblk)]
+    products, squares = [], []
     for n, (h, c) in enumerate(at):
-        kb[h, c] = keys[n]
-        norm[first * nblk + n] = rrows[n]
-        lower = jnp.where(row > col, products[n] * (2.0 * rcols[n] * rcols[n]), 0.0)
+        key = kf[pl.ds(c * BLK * heads + h, BLK, stride=heads), :].astype(BF16)
+        kb[h, c] = key
+        products.append(dot_bt(key, key))
+        yield
+    for n, gram in enumerate(products):
+        diag = jnp.where(eye, gram, 0.0)
+        squares.append(jnp.sum(diag, axis=1, keepdims=True))
+        norm[first * nblk + n] = lax.rsqrt(jnp.sum(diag, axis=0, keepdims=True) + 1e-6)
+        yield
+    for n, gram in enumerate(products):
+        rcol = lax.rsqrt(squares[n] + 1e-6)
+        lower = jnp.where(row > col, gram * (2.0 * rcol * rcol), 0.0)
         low[first * nblk + n] = lower
         packed = lower[:SUB]
         for g in range(1, BLK // SUB):
             packed = jnp.where(lane // SUB == g, lower[g * SUB : (g + 1) * SUB], packed)
         dsc[pl.ds(pl.multiple_of((first * nblk + n) * SUB, SUB), SUB), :] = packed
-
-
-def substitute(count, dsc, nsc):
+        yield
+
+
+def substitute(first, count, dsc, nsc):
     lane = iota((count, BLK), 1)
     solved = []
     for i in range(SUB):
-        line = dsc[pl.ds(i, count, stride=SUB), :]
+        line = dsc[pl.ds(first * SUB + i, count, stride=SUB), :]
         total = jnp.where(lane % SUB == i, 1.0, 0.0)
         for j in range(i):
             factor = jnp.take_along_axis(line, (lane // SUB) * SUB + j, axis=1)
             total = total - factor * solved[j]
         solved.append(total)
-        nsc[pl.ds(i, count, stride=SUB), :] = total
-
-
-def factors(first, per, heads, nblk, vf, nsc, low, norm, kb, steps, scaled_hi, scaled_lo, before, both, core):
+        nsc[pl.ds(first * SUB + i, count, stride=SUB), :] = total
+        yield
+
+
+def factors(beside, first, per, heads, nblk, vf, nsc, low, norm, kb, steps, scaled_hi, scaled_lo, before, both, core):
     dk = kb.shape[-1]
     eye = iota((BLK, BLK), 0) == iota((BLK, BLK), 1)
     lane = iota((SUB, BLK), 1)
@@ -156,8 +162,13 @@
         )
     size = SUB
     while size < BLK:
-        inverses = [invert_level(inv, low[base + n], size) for n, inv in enumerate(inverses)]
+        for n in range(per * nblk):
+            inverses[n] = invert_level(inverses[n], low[base + n], size)
+            for _ in range(2):
+                next(beside, None)
         size *= 2
+    for _ in beside:
+        pass
 
     count = per * nblk
     at = [(first + n // nblk, n % nblk) for n in range(count)]
@@ -326,24 +337,25 @@
     loads[0].wait()
     kf[...] = k_ref[...].astype(F32)
 
-    def gramming(i, _):
-        grams(i * per, per, heads, nblk, kf, dsc, low, norm, kb)
-        return 0
-
-    lax.fori_loop(0, heads // per, gramming, 0)
-    substitute(heads * nblk, dsc, nsc)
+    def group_of(i):
+        turn = lax.rem(i + 1 + mine // per, heads // per)
+        return turn, [turn * per + lax.rem(mine + 1 + d, per) for d in range(per)]
+
+    def prepared(first):
+        yield from grams(first, per, heads, nblk, kf, dsc, low, norm, kb)
+        yield from substitute(first * nblk, per * nblk, dsc, nsc)
+
+    for _ in prepared(group_of(0)[0] * per):
+        pass
+
     for load in loads[1:]:
         load.wait()
     vf[...] = v_ref[...].astype(F32)
-    qf[...] = q_ref[...].astype(F32)
-
-    def group_of(i):
-        turn = lax.rem(i + 1 + mine // per, heads // per)
-        return turn, [turn * per + lax.rem(mine + 1 + d, per) for d in range(per)]
 
     def local(i, _):
         turn, group = group_of(i)
-        factors(turn * per, per, heads, nblk, vf, nsc, low, norm, kb, steps, scaled_hi, scaled_lo, before, both, core)
+        beside = prepared(group_of(i + 1)[0] * per)
+        factors(beside, turn * per, per, heads, nblk, vf, nsc, low, norm, kb, steps, scaled_hi, scaled_lo, before, both, core)
 
         @pl.when(i == 0)
         def _():
@@ -358,9 +370,7 @@
 
     lax.fori_loop(0, heads // per, local, 0)
 
-    def merging(i, _):
-        _, group = group_of(i)
-
+    def merging(group):
         def arrived(c):
             for h in group:
                 mput(h, 1 - c).wait_recv()
@@ -378,9 +388,19 @@
             def _():
                 rx[chip, mine_rows] = merged[h]
 
+    def merging_all(i, _):
+        merging(group_of(i)[1])
         return 0
 
-    lax.fori_loop(0, heads // per, merging, 0)
+    lax.fori_loop(0, heads // per - 1, merging_all, 0)
+
+    def merging_one(d, _):
+        merging([group_of(heads // per - 1)[0] * per + lax.rem(mine + 1 + d, per)])
+        return 0
+
+    lax.fori_loop(0, per, merging_one, 0)
+
+    qf[...] = q_ref[...].astype(F32)
 
     def reading(h, _):
         readers(h, heads, nblk, qf, kb, steps, scaled_hi, scaled_lo, before, reach, base)
@@ -480,6 +500,31 @@
 
         lax.fori_loop(0, chips, give, 0)
 
+    def sent(c):
+        for h in range(heads):
+            mput(h, c).wait_send()
+
+    for_core(sent)
+
+    for h in range(heads):
+
+        @pl.when(me != h * span)
+        def _():
+            put(h).wait_send()
+
+    @pl.when(owner)
+    def _():
+        @pl.when(seg == 0)
+        def _():
+            for g in range(1, segs):
+                fput(g).wait_send()
+
+        for g in range(2, segs):
+
+            @pl.when((seg > 0) & (seg < g))
+            def _():
+                zput(g).wait_send()
+
     def ordered(k):
         return lax.rem(mine + (k // per) + (k % per) * (heads // per), heads)
 
@@ -525,17 +570,7 @@
     lax.fori_loop(0, heads // 2, closing, 0)
     out_ref[...] = qf[...].astype(BF16)
 
-    def sent(c):
-        for h in range(heads):
-            mput(h, c).wait_send()
-
-    for_core(sent)
-
     for h in range(heads):
-
-        @pl.when(me != h * span)
-        def _():
-            put(h).wait_send()
 
         @pl.when((core == 0) & relayed(h))
         def _():
@@ -543,17 +578,6 @@
 
     @pl.when(owner)
     def _():
-        @pl.when(seg == 0)
-        def _():
-            for g in range(1, segs):
-                fput(g).wait_send()
-
-        for g in range(2, segs):
-
-            @pl.when((seg > 0) & (seg < g))
-            def _():
-                zput(g).wait_send()
-
         def done(s, _):
             @pl.when(s != chip)
             def _():

time: 26.7 us -> 26.4 us (0.989)
  Pallas kernels: 25.8 us -> 25.5 us
    pallas_call x1, Pallas kernels: 25.8 us -> 25.5 us  [per_device(): pl.pallas_call(functools.partial(kernel, seqs, segs, heads, per), in_spec...]
where the time goes in v5:
time: 26.4 us; the launch traced here: 26.3 us
  Pallas kernels  25.5 us (97%)
  local copies, waits for them, and re-layouts  0.71 us (3%)
    pallas_call x1, Pallas kernels, per_device(): pl.pallas_call(functools.partial(kernel, seqs, segs, heads, per), in_spec...  25.5 us
    unnamed x1, local copies, waits for them, and re-layouts  0.71 us

profile of v5, /device:TPU:17, one launch (start us, length us, event | category | flops | bytes accessed | tf_op | source)
XLA Modules:
  0.0 26.3 jit_solution(8022076833015257657)
XLA Ops:
  0.0 25.5 %delta_product.1 = bf16[1024,128]{1,0:T(8,128)(2,1)S(1)} custom-call(bf16[1024,128]{1,0:T(8,128)(2,1)} %bitcast.7, bf16[2048,128]{1,0:T(8,128)(2,1)} %bitcast.5, bf16[2048,128]{1,0:T(8,128)(2,1)} %bitcast.6, f32[4,128]{1,0:T(4,128)} %gain_any.1, f32[4,128,128]{2,1,0:T(8,128)} %init_any.1), custom_call_target="tpu_custom_call" | custom-call | tf_op jit(solution)/shard_map/delta_product/pallas_call | solution.py:607
  25.6 0.7 %copy.7 = bf16[1,256,4,128]{3,2,1,0:T(4,128)(2,1)} copy(bf16[1,256,4,128]{3,2,1,0:T(4,128)(2,1)S(1)} %bitcast.4) | data formatting | bytes 524288

commit v6 on v5

--- a/solution.py
+++ b/solution.py
@@ -354,8 +354,15 @@
 
     def local(i, _):
         turn, group = group_of(i)
-        beside = prepared(group_of(i + 1)[0] * per)
-        factors(beside, turn * per, per, heads, nblk, vf, nsc, low, norm, kb, steps, scaled_hi, scaled_lo, before, both, core)
+        @pl.when(i + 1 < heads // per)
+        def _():
+            beside = prepared(group_of(i + 1)[0] * per)
+            factors(beside, turn * per, per, heads, nblk, vf, nsc, low, norm, kb, steps, scaled_hi, scaled_lo, before, both, core)
+
+        @pl.when(i + 1 == heads // per)
+        def _():
+            beside = iter(())
+            factors(beside, turn * per, per, heads, nblk, vf, nsc, low, norm, kb, steps, scaled_hi, scaled_lo, before, both, core)
 
         @pl.when(i == 0)
         def _():

time: 26.4 us -> 26.2 us (level)
  no operation moved by 1% of the time
where the time goes in v6:
time: 26.2 us; the launch traced here: 26.1 us
  Pallas kernels  25.4 us (97%)
  local copies, waits for them, and re-layouts  0.71 us (3%)
    pallas_call x1, Pallas kernels, per_device(): pl.pallas_call(functools.partial(kernel, seqs, segs, heads, per), in_spec...  25.4 us
    unnamed x1, local copies, waits for them, and re-layouts  0.71 us

profile of v6, /device:TPU:17, one launch (start us, length us, event | category | flops | bytes accessed | tf_op | source)
XLA Modules:
  0.0 26.1 jit_solution(5103567432649238991)
XLA Ops:
  0.0 25.4 %delta_product.1 = bf16[1024,128]{1,0:T(8,128)(2,1)S(1)} custom-call(bf16[1024,128]{1,0:T(8,128)(2,1)} %bitcast.7, bf16[2048,128]{1,0:T(8,128)(2,1)} %bitcast.5, bf16[2048,128]{1,0:T(8,128)(2,1)} %bitcast.6, f32[4,128]{1,0:T(4,128)} %gain_any.1, f32[4,128,128]{2,1,0:T(8,128)} %init_any.1), custom_call_target="tpu_custom_call" | custom-call | tf_op jit(solution)/shard_map/delta_product/pallas_call | solution.py:614
  25.4 0.7 %copy.7 = bf16[1,256,4,128]{3,2,1,0:T(4,128)(2,1)} copy(bf16[1,256,4,128]{3,2,1,0:T(4,128)(2,1)S(1)} %bitcast.4) | data formatting | bytes 524288

commit v7 on v6

--- a/solution.py
+++ b/solution.py
@@ -487,7 +487,8 @@
                 state[...] = applied(zx[g], state[...])
 
         def give(k, _):
-            s = lax.rem(2 * chips - 1 - chip + k, chips)
+            turn = lax.rem(chip, 2) + (chips - 1) * (1 - lax.rem(chip, 2))
+            s = lax.rem(chips - 1 - chip + k * turn, chips)
             ready = applied(prefix[s], state[...])
 
             @pl.when(s != chip)

time: 26.2 us -> 26.2 us (level)
  no operation moved by 1% of the time
where the time goes in v7:
time: 26.2 us; the launch traced here: 26.1 us
  Pallas kernels  25.4 us (97%)
  local copies, waits for them, and re-layouts  0.71 us (3%)
    pallas_call x1, Pallas kernels, per_device(): pl.pallas_call(functools.partial(kernel, seqs, segs, heads, per), in_spec...  25.4 us
    unnamed x1, local copies, waits for them, and re-layouts  0.71 us

profile of v7, /device:TPU:17, one launch (start us, length us, event | category | flops | bytes accessed | tf_op | source)
XLA Modules:
  0.0 26.1 jit_solution(14575275073587322385)
XLA Ops:
  0.0 25.4 %delta_product.1 = bf16[1024,128]{1,0:T(8,128)(2,1)S(1)} custom-call(bf16[1024,128]{1,0:T(8,128)(2,1)} %bitcast.7, bf16[2048,128]{1,0:T(8,128)(2,1)} %bitcast.5, bf16[2048,128]{1,0:T(8,128)(2,1)} %bitcast.6, f32[4,128]{1,0:T(4,128)} %gain_any.1, f32[4,128,128]{2,1,0:T(8,128)} %init_any.1), custom_call_target="tpu_custom_call" | custom-call | tf_op jit(solution)/shard_map/delta_product/pallas_call | solution.py:615
  25.4 0.7 %copy.7 = bf16[1,256,4,128]{3,2,1,0:T(4,128)(2,1)} copy(bf16[1,256,4,128]{3,2,1,0:T(4,128)(2,1)S(1)} %bitcast.4) | data formatting | bytes 524288

commit v8 on v7

--- a/solution.py
+++ b/solution.py
@@ -453,7 +453,7 @@
             for g in range(segs - 1, 0, -1):
                 fput(g).start()
 
-        for g in range(segs - 1, 1, -1):
+        for g in range(2, segs):
 
             @pl.when((seg > 0) & (seg < g))
             def _():

time: 26.2 us -> 26.2 us (level)
  the two profiles are of different devices: /device:TPU:17 before, /device:TPU:25 now
where the time goes in v8:
time: 26.2 us; the launch traced here: 26.1 us
  Pallas kernels  25.4 us (97%)
  local copies, waits for them, and re-layouts  0.71 us (3%)
    pallas_call x1, Pallas kernels, per_device(): pl.pallas_call(functools.partial(kernel, seqs, segs, heads, per), in_spec...  25.4 us
    unnamed x1, local copies, waits for them, and re-layouts  0.71 us

profile of v8, /device:TPU:25, one launch (start us, length us, event | category | flops | bytes accessed | tf_op | source)
XLA Modules:
  0.0 26.1 jit_solution(11648573830553532990)
XLA Ops:
  0.0 25.4 %delta_product.1 = bf16[1024,128]{1,0:T(8,128)(2,1)S(1)} custom-call(bf16[1024,128]{1,0:T(8,128)(2,1)} %bitcast.7, bf16[2048,128]{1,0:T(8,128)(2,1)} %bitcast.5, bf16[2048,128]{1,0:T(8,128)(2,1)} %bitcast.6, f32[4,128]{1,0:T(4,128)} %gain_any.1, f32[4,128,128]{2,1,0:T(8,128)} %init_any.1), custom_call_target="tpu_custom_call" | custom-call | tf_op jit(solution)/shard_map/delta_product/pallas_call | solution.py:615
  25.4 0.7 %copy.7 = bf16[1,256,4,128]{3,2,1,0:T(4,128)(2,1)} copy(bf16[1,256,4,128]{3,2,1,0:T(4,128)(2,1)S(1)} %bitcast.4) | data formatting | bytes 524288
